TPU v7x, 128 devices: a whole 4x4x4 slice. The times are simulated.
128 devices in a mesh: psg: 32 (over y, z, core), qry: 4 (over x).
Axes of the slice: x: 4, y: 4, z: 4, core: 2. Of those that a mesh axis runs over, the one named last changes fastest.
Arguments:
- queries: bfloat16 [512, 32, 128], P(('psg', 'qry')), may hold values from -6 to 6
- passages: bfloat16 [1024, 256, 128], P('psg'), may hold values from -6 to 6
- candidates: int32 [512, 32], P(('psg', 'qry')), may hold values from 0 to 1023, as said below
- teacher: float32 [512, 32], P(('psg', 'qry')), may hold values from -8 to 8
Outputs:
- pair_loss: float32 [512], P(('psg', 'qry'))
- grad_queries: bfloat16 [512, 32, 128], P(('psg', 'qry'))
- grad_passages: bfloat16 [1024, 256, 128], P('psg', 'qry')
Inputs may be any that keep to these rules, and one draw needn't show every extreme that they name: Passage p lies in block p // 32. Among the 4 x 32 candidates of one device's queries (aligned blocks of 4 rows), at most 10 lie in one passage block; one passage block, the same for all devices, holds exactly 10 of every device's candidates. Candidate ids of one query may repeat.
All inputs are finite; a program needn't handle non-finite values.
Results may differ from a plain program's by a relative error of at most 0.019.
Values may be sent and summed in bfloat16 or wider, within the bound.
A program may use at most 64 MiB of HBM per device.

v0:
```python
import math
import jax
import jax.numpy as jnp
from jax import lax
from jax.sharding import PartitionSpec as P

epsilon = 1e-06
softness_scale = 0.05


def normalize(values):
    widened = values.astype(jnp.float32)
    inverse_norm = lax.rsqrt(jnp.sum(widened * widened, -1, keepdims=True) + epsilon)
    return (widened * inverse_norm, inverse_norm)


def select_rows(row_ids, table):
    row_total = table.shape[0]
    picker = (row_ids[:, None] == lax.iota(jnp.int32, row_total)[None, :]).astype(jnp.bfloat16)
    flat_table = table.reshape(row_total, -1)
    chosen = jnp.dot(picker, flat_table, preferred_element_type=jnp.float32).astype(jnp.bfloat16)
    return chosen.reshape((row_ids.shape[0],) + table.shape[1:])


def add_rows(accum, row_ids, delta):
    row_total = accum.shape[0]
    placer = (row_ids[:, None] == lax.iota(jnp.int32, row_total)[None, :]).astype(jnp.float32)
    flat_delta = delta.reshape(row_ids.shape[0], -1)
    added = jnp.einsum("sr,sx->rx", placer, flat_delta, precision=lax.Precision.HIGHEST)
    return accum + added.reshape(accum.shape)


def shards(queries, passages, candidates, teacher):
    query_count, query_tokens, feature_count = queries.shape
    pass_count, passage_tokens, _ = passages.shape
    cand_count = candidates.shape[1]
    owner_count = lax.axis_size("psg")
    capacity = max(2, (5 * query_count * cand_count + 2 * owner_count - 1) // (2 * owner_count))
    slot_count = owner_count * capacity
    pair_count = query_count * cand_count
    query_unit, query_inverse = normalize(queries)
    passage_unit, passage_inverse = normalize(passages)
    query_norm = query_unit.astype(jnp.bfloat16)
    passage_norm = passage_unit.astype(jnp.bfloat16)
    owner_ids = (candidates // pass_count).reshape(-1)
    local_ids = (candidates % pass_count).reshape(-1)
    onehot = (owner_ids[:, None] == lax.iota(jnp.int32, owner_count)[None, :]).astype(jnp.int32)
    before = jnp.cumsum(onehot, 0) - onehot
    rank_in_owner = jnp.sum(before * onehot, 1)
    slot_ids = owner_ids * capacity + rank_in_owner
    query_local = lax.iota(jnp.int32, pair_count) // cand_count
    slot_code = (
        jnp.zeros((slot_count,), jnp.int32)
        .at[slot_ids]
        .set(query_local * pass_count + local_ids + 1)
    )
    send_code = slot_code.reshape(owner_count, capacity)
    sender = lax.iota(jnp.int32, slot_count) // capacity
    received_label = lax.all_to_all(send_code, "psg", split_axis=0, concat_axis=0, tiled=True)
    query_rows = lax.all_gather(query_norm, "psg", axis=0, tiled=True)
    flat_peek = received_label.reshape(-1)
    fetch_rows = sender * query_count + jnp.where(flat_peek > 0, (flat_peek - 1) // pass_count, 0)
    flat_code = received_label.reshape(-1)
    live = flat_code > 0
    pass_index = jnp.where(live, (flat_code - 1) % pass_count, 0)
    target_rows = sender * query_count + jnp.where(live, (flat_code - 1) // pass_count, 0)
    block_len = math.gcd(slot_count, 64)
    block_total = slot_count // block_len

    def block_terms(offset):
        row_ids = lax.dynamic_slice_in_dim(fetch_rows, offset, block_len)
        passage_ids = lax.dynamic_slice_in_dim(pass_index, offset, block_len)
        query_tile = select_rows(row_ids, query_rows)
        passage_tile = select_rows(passage_ids, passage_norm)
        token_products = jnp.einsum(
            "sqe,spe->sqp", query_tile, passage_tile, preferred_element_type=jnp.float32
        )
        power_value = jnp.exp(token_products / softness_scale)
        return (query_tile, passage_tile, passage_ids, power_value, jnp.sum(power_value, -1))

    def forward_block(offset):
        reduced_sum = block_terms(offset)[4]
        return jnp.sum(softness_scale * jnp.log(reduced_sum), -1)

    offsets = lax.iota(jnp.int32, block_total) * block_len
    slot_scores = lax.map(forward_block, offsets).reshape(owner_count, capacity)
    scores_home = lax.all_to_all(slot_scores, "psg", split_axis=0, concat_axis=0, tiled=True)
    scores = scores_home.reshape(-1)[slot_ids].reshape(query_count, cand_count)
    teacher_exp = jnp.exp(teacher)
    mentor_score_sum = jnp.sum(teacher_exp, -1, keepdims=True)
    target = teacher_exp / mentor_score_sum
    log_target = teacher - jnp.log(mentor_score_sum)
    score_exp = jnp.exp(scores)
    score_total = jnp.sum(score_exp, -1, keepdims=True)
    likelihood = score_exp / score_total
    pair_loss = jnp.sum(target * (log_target - scores), -1) + jnp.log(score_total[:, 0])
    score_grad = likelihood - target
    send_grad = jnp.zeros((slot_count,), jnp.float32).at[slot_ids].set(score_grad.reshape(-1))
    recv_grad = lax.all_to_all(
        send_grad.reshape(owner_count, capacity), "psg", split_axis=0, concat_axis=0, tiled=True
    )
    flat_grad = recv_grad.reshape(-1)

    def backward(step_index, running):
        query_accum, passage_accum = running
        offset = step_index * block_len
        query_tile, passage_tile, passage_ids, power_value, reduced_sum = block_terms(offset)
        slot_grad = lax.dynamic_slice_in_dim(flat_grad, offset, block_len)
        weights = (slot_grad[:, None, None] * power_value / reduced_sum[:, :, None]).astype(
            jnp.bfloat16
        )
        query_delta = jnp.einsum(
            "sqp,spe->sqe", weights, passage_tile, preferred_element_type=jnp.float32
        )
        passage_delta = jnp.einsum(
            "sqp,sqe->spe", weights, query_tile, preferred_element_type=jnp.float32
        )
        home_rows = lax.dynamic_slice_in_dim(target_rows, offset, block_len)
        return (
            add_rows(query_accum, home_rows, query_delta),
            add_rows(passage_accum, passage_ids, passage_delta),
        )

    start_state = (
        jnp.zeros((owner_count * query_count, query_tokens, feature_count), jnp.float32),
        jnp.zeros((pass_count, passage_tokens, feature_count), jnp.float32),
    )
    query_accum, passage_accum = lax.fori_loop(0, block_total, backward, start_state)
    unit_query_grad = lax.psum_scatter(
        query_accum.astype(jnp.bfloat16), "psg", scatter_dimension=0, tiled=True
    ).astype(jnp.float32)
    unit_passage_grad = lax.psum_scatter(
        passage_accum.astype(jnp.bfloat16), "qry", scatter_dimension=1, tiled=True
    ).astype(jnp.float32)
    token_share = unit_passage_grad.shape[1]
    shard_start = lax.axis_index("qry") * token_share
    unit_slice = lax.dynamic_slice_in_dim(passage_unit, shard_start, token_share, 1)
    inverse_slice = lax.dynamic_slice_in_dim(passage_inverse, shard_start, token_share, 1)
    grad_queries = query_inverse * (
        unit_query_grad - query_unit * jnp.sum(query_unit * unit_query_grad, -1, keepdims=True)
    )
    grad_passages = inverse_slice * (
        unit_passage_grad - unit_slice * jnp.sum(unit_slice * unit_passage_grad, -1, keepdims=True)
    )
    return (pair_loss, grad_queries.astype(jnp.bfloat16), grad_passages.astype(jnp.bfloat16))


def solution(mesh):
    placed = (
        P(("psg", "qry"), None, None),
        P("psg", None, None),
        P(("psg", "qry"), None),
        P(("psg", "qry"), None),
    )
    return jax.shard_map(
        shards,
        mesh=mesh,
        in_specs=placed,
        out_specs=(P(("psg", "qry")), P(("psg", "qry"), None, None), P("psg", "qry", None)),
        check_vma=False,
    )
```

profile of v0, /device:TPU:1, one launch (start us, length us, event | category | flops | bytes accessed | tf_op | source)
XLA Modules:
  0.0 386.0 jit_solution(9751753425798929386)
XLA Ops:
  12.7 9.6 %all-to-all-start = ((s32[32,1,10]{2,1,0:T(1,128)}), s32[32,1,10]{2,1,0:T(1,128)S(1)}, u32[]{:S(2)}, u32[]{:S(2)}) async-start(s32[32,1,10]{2,1,0:T(1,128)} %bitcast.4), calls=%async_computation | async-start | bytes 32768 | tf_op jit(solution)/shard_map/all_to_all | solution.py:59
  22.3 2.9 fusion.34
  25.2 3.1 convert_multiply_fusion
  29.5 27.6 %all-gather.2.cloned.1.call-done = bf16[128,32,128]{2,1,0:T(8,128)(2,1)} async-done(((bf16[4,32,128]{2,1,0:T(8,128)(2,1)}), bf16[128,32,128]{2,1,0:T(8,128)(2,1)}) %all-gather.2.cloned.1.call-update) | async-done | bytes 1048592 | tf_op jit(solution)/shard_map/all_gather | solution.py:60
  57.1 44.8 %while.27 = (s32[]{:T(128)}, f32[5,64]{1,0:T(8,128)S(1)}, s32[5]{0:T(128)S(1)}, s32[320]{0:T(512)S(1)}, bf16[128,32,128]{2,1,0:T(8,128)(2,1)}, /*index=5*/s32[32...) while((s32[]{:T(128)}, f32[5,64]{1,0:T(8,128)S(1)}, s32[5]{0:T(128)S(1)}, ...), condition=%wide.region_9.10_spmd, body=%wide.region_6.9_spmd.sunk | while | flops 338964416 | bytes 22055336 | solution.py:86
  102.6 5.3 %all-to-all-start.1 = ((f32[32,1,10]{2,1,0:T(1,128)}), f32[32,1,10]{2,1,0:T(1,128)S(1)}, u32[]{:S(2)}, u32[]{:S(2)}) async-start(f32[32,1,10]{2,1,0:T(1,128)} %bitcast.5), calls=%async_computation.1 | async-start | bytes 32768 | tf_op jit(solution)/shard_map/all_to_all | solution.py:87
  108.1 6.8 %all-to-all-done.1 = f32[32,1,10]{2,1,0:T(1,128)S(1)} async-done(((f32[32,1,10]{2,1,0:T(1,128)}), f32[32,1,10]{2,1,0:T(1,128)S(1)}, u32[]{:S(2)}, u32[]{:S(2)}) %all-to-all-start.1) | async-done | bytes 1312 | tf_op jit(solution)/shard_map/all_to_all | solution.py:87
  119.6 4.1 %all-to-all-start.2 = ((f32[32,1,10]{2,1,0:T(1,128)}), f32[32,1,10]{2,1,0:T(1,128)S(1)}, u32[]{:S(2)}, u32[]{:S(2)}) async-start(f32[32,1,10]{2,1,0:T(1,128)} %bitcast.6), calls=%async_computation.2 | async-start | bytes 32768 | tf_op jit(solution)/shard_map/all_to_all | solution.py:99
  123.8 6.9 %all-to-all-done.2 = f32[32,1,10]{2,1,0:T(1,128)S(1)} async-done(((f32[32,1,10]{2,1,0:T(1,128)}), f32[32,1,10]{2,1,0:T(1,128)S(1)}, u32[]{:S(2)}, u32[]{:S(2)}) %all-to-all-start.2) | async-done | bytes 1312 | tf_op jit(solution)/shard_map/all_to_all | solution.py:99
  131.5 131.0 %while.28 = (s32[]{:T(128)}, f32[128,32,128]{2,0,1:T(8,128)}, f32[32,256,128]{2,0,1:T(8,128)}, s32[320]{0:T(512)S(1)}, f32[320]{0:T(512)S(1)}, /*index=5*/bf16[1...) while((s32[]{:T(128)}, f32[128,32,128]{2,0,1:T(8,128)}, ...), condition=%wide.region_15.16_spmd.clone, body=%wide.region_13.15_spmd.clone.sunk | while | flops 1822705664 | bytes 114847024 | solution.py:128
  145.3 10.6 %select_add_fusion.5 = f32[32,256,128]{2,0,1:T(8,128)S(1)} fusion(f32[32,256,128]{2,0,1:T(8,128)S(1)} %copy-done, pred[]{:T(512)S(6)} %compare.11, s32[64]{0:T(128)S(1)} %dynamic_slice.59, f32[8,8,256,128]{3,2,1,0:T(8,128)S(1)} %bitcast.149), kind=kOutput, calls=%fused_computation.23.clone.1 | convolution fusion | flops 807405568 | bytes 16777472 | tf_op jit(solution)/shard_map/while/body/eval_jaxpr/sr,sx->rx/dot_general | solution.py:29
  165.8 2.7 select_add_fusion.4
  171.4 10.6 %select_add_fusion.5 = f32[32,256,128]{2,0,1:T(8,128)S(1)} fusion(f32[32,256,128]{2,0,1:T(8,128)S(1)} %copy-done, pred[]{:T(512)S(6)} %compare.11, s32[64]{0:T(128)S(1)} %dynamic_slice.59, f32[8,8,256,128]{3,2,1,0:T(8,128)S(1)} %bitcast.149), kind=kOutput, calls=%fused_computation.23.clone.1 | convolution fusion | flops 807405568 | bytes 16777472 | tf_op jit(solution)/shard_map/while/body/eval_jaxpr/sr,sx->rx/dot_general | solution.py:29
  192.0 2.7 select_add_fusion.4
  197.6 10.6 %select_add_fusion.5 = f32[32,256,128]{2,0,1:T(8,128)S(1)} fusion(f32[32,256,128]{2,0,1:T(8,128)S(1)} %copy-done, pred[]{:T(512)S(6)} %compare.11, s32[64]{0:T(128)S(1)} %dynamic_slice.59, f32[8,8,256,128]{3,2,1,0:T(8,128)S(1)} %bitcast.149), kind=kOutput, calls=%fused_computation.23.clone.1 | convolution fusion | flops 807405568 | bytes 16777472 | tf_op jit(solution)/shard_map/while/body/eval_jaxpr/sr,sx->rx/dot_general | solution.py:29
  218.1 2.7 select_add_fusion.4
  223.7 10.6 %select_add_fusion.5 = f32[32,256,128]{2,0,1:T(8,128)S(1)} fusion(f32[32,256,128]{2,0,1:T(8,128)S(1)} %copy-done, pred[]{:T(512)S(6)} %compare.11, s32[64]{0:T(128)S(1)} %dynamic_slice.59, f32[8,8,256,128]{3,2,1,0:T(8,128)S(1)} %bitcast.149), kind=kOutput, calls=%fused_computation.23.clone.1 | convolution fusion | flops 807405568 | bytes 16777472 | tf_op jit(solution)/shard_map/while/body/eval_jaxpr/sr,sx->rx/dot_general | solution.py:29
  244.3 2.7 select_add_fusion.4
  249.9 10.6 %select_add_fusion.5 = f32[32,256,128]{2,0,1:T(8,128)S(1)} fusion(f32[32,256,128]{2,0,1:T(8,128)S(1)} %copy-done, pred[]{:T(512)S(6)} %compare.11, s32[64]{0:T(128)S(1)} %dynamic_slice.59, f32[8,8,256,128]{3,2,1,0:T(8,128)S(1)} %bitcast.149), kind=kOutput, calls=%fused_computation.23.clone.1 | convolution fusion | flops 807405568 | bytes 16777472 | tf_op jit(solution)/shard_map/while/body/eval_jaxpr/sr,sx->rx/dot_general | solution.py:29
  262.5 3.8 copy.86
  266.3 6.0 %copy.85 = bf16[32,256,128]{2,1,0:T(8,128)(2,1)} copy(f32[32,256,128]{2,0,1:T(8,128)} %get-tuple-element.206) | data formatting | bytes 6291456 | tf_op jit(solution)/shard_map/while | solution.py:128
  273.0 67.0 %reduce-scatter.3.cloned.1.call-done = bf16[4,32,128]{2,1,0:T(8,128)(2,1)} async-done(((bf16[128,32,128]{2,1,0:T(8,128)(2,1)}), bf16[4,32,128]{2,1,0:T(8,128)(2,1)}) %reduce-scatter.3.cloned.1.call-update) | async-done | bytes 32784 | tf_op jit(solution)/shard_map/reduce_scatter | solution.py:129
  342.0 31.2 %reduce-scatter.5.cloned.1.call-done = bf16[32,64,128]{2,1,0:T(8,128)(2,1)} async-done(((bf16[32,256,128]{2,1,0:T(8,128)(2,1)}), bf16[32,64,128]{2,1,0:T(8,128)(2,1)}) %reduce-scatter.5.cloned.1.call-update) | async-done | bytes 524304 | tf_op jit(solution)/shard_map/reduce_scatter | solution.py:132
  373.2 6.3 %fusion.39 = bf16[32,64,128]{2,1,0:T(8,128)(2,1)} fusion(bf16[32,64,128]{2,1,0:T(8,128)(2,1)} %reduce-scatter.5.cloned.1.call-done, f32[32,256,128]{2,1,0:T(8,128)} %get-tuple-element.270, s32[]{:T(128)S(6)} %select_n.80, f32[32,64]{1,0:T(8,128)S(1)} %constant_dynamic-slice_fusion), kind=kOutput, calls=%fused_computation.59 | output fusion | flops 1837183 | bytes 3679232 | tf_op jit(solution)/shard_map/mul | solution.py:143
  (202 shorter events, 117.1 us)
Async XLA Ops:
  7.2 50.0 %all-gather.2.cloned.1.call-start = ((), (), s32[]{:S(2)}) async-start(), calls=%async_computation.5 | async-start | bytes 1081344 | tf_op jit(solution)/shard_map/all_gather | solution.py:60
  12.7 16.5 %all-to-all-start = ((s32[32,1,10]{2,1,0:T(1,128)}), s32[32,1,10]{2,1,0:T(1,128)S(1)}, u32[]{:S(2)}, u32[]{:S(2)}) async-start(s32[32,1,10]{2,1,0:T(1,128)} %bitcast.4), calls=%async_computation | async-start | bytes 32768 | tf_op jit(solution)/shard_map/all_to_all | solution.py:59
  22.3 3.0 copy-start.4
  57.1 50.8 %copy-start.6 = (f32[4,32]{1,0:T(4,128)S(1)}, f32[4,32]{1,0:T(4,128)}, u32[]{:S(2)}) copy-start(f32[4,32]{1,0:T(4,128)} %param.11) | copy-start | bytes 1540
  102.6 12.2 %all-to-all-start.1 = ((f32[32,1,10]{2,1,0:T(1,128)}), f32[32,1,10]{2,1,0:T(1,128)S(1)}, u32[]{:S(2)}, u32[]{:S(2)}) async-start(f32[32,1,10]{2,1,0:T(1,128)} %bitcast.5), calls=%async_computation.1 | async-start | bytes 32768 | tf_op jit(solution)/shard_map/all_to_all | solution.py:87
  119.6 11.2 %all-to-all-start.2 = ((f32[32,1,10]{2,1,0:T(1,128)}), f32[32,1,10]{2,1,0:T(1,128)S(1)}, u32[]{:S(2)}, u32[]{:S(2)}) async-start(f32[32,1,10]{2,1,0:T(1,128)} %bitcast.6), calls=%async_computation.2 | async-start | bytes 32768 | tf_op jit(solution)/shard_map/all_to_all | solution.py:99
  123.7 216.3 %reduce-scatter.3.cloned.1.call-start = ((), (), s32[]{:S(2)}) async-start(), calls=%async_computation.6 | async-start | bytes 1081344 | tf_op jit(solution)/shard_map/reduce_scatter | solution.py:129
  142.3 1.9 copy-start.3
  142.3 2.9 copy-start
  155.9 2.0 copy-start.1
  168.5 1.9 copy-start.3
  168.5 2.9 copy-start
  182.0 2.0 copy-start.1
  194.6 1.9 copy-start.3
  194.6 2.9 copy-start
  208.2 2.0 copy-start.1
  220.8 1.9 copy-start.3
  220.8 2.9 copy-start
  234.4 2.0 copy-start.1
  246.9 1.9 copy-start.3
  246.9 2.9 copy-start
  260.5 2.0 copy-start.1
  266.3 106.9 %reduce-scatter.5.cloned.1.call-start = ((), (), s32[]{:S(2)}) async-start(), calls=%async_computation.7 | async-start | bytes 2621440 | tf_op jit(solution)/shard_map/reduce_scatter | solution.py:132
  272.4 67.7 %copy-start.5 = (bf16[4,32,128]{2,1,0:T(8,128)(2,1)S(1)}, bf16[4,32,128]{2,1,0:T(8,128)(2,1)}, u32[]{:S(2)}) copy-start(bf16[4,32,128]{2,1,0:T(8,128)(2,1)} %param.8) | copy-start | bytes 98308
  (5 other events, 8.0 us)
Sparse Core Ops, SparseCore 0:
  10.8 46.2 all-gather.1
  266.4 73.5 reduce-scatter.2
  342.4 30.7 reduce-scatter.4
where the time goes:
time: 388 us; the launch traced here: 386 us
  waiting for transfers between devices  140 us (36%)
  matrix products  129 us (33%)
  local copies, waits for them, and re-layouts  53 us (14%)
  other arithmetic  20.3 us (5%)
  starting transfers between devices  19.1 us (5%)
  between operations  14 us (4%)
  loops' own time  10.6 us (3%)
    reduce_scatter x1, waiting for transfers between devices, shards(): lax.psum_scatter(query_accum.astype(jnp.bfloat16), 'psg', scatter_dimensi...  67 us
    dot_general x10, matrix products, add_rows(): jnp.einsum('sr,sx->rx', placer, flat_delta, precision=lax.Precision.HIGHEST)  66.4 us
    dot_general x20, matrix products, select_rows(): jnp.dot(picker, flat_table, preferred_element_type=jnp.float32)  32.2 us
    reduce_scatter x1, waiting for transfers between devices, shards(): lax.psum_scatter(passage_accum.astype(jnp.bfloat16), 'qry', scatter_dimen...  31.2 us
    while x60, local copies, waits for them, and re-layouts  31.1 us
    all_gather x1, waiting for transfers between devices, shards(): query_rows = lax.all_gather(query_norm, 'psg', axis=0, tiled=True)  27.6 us
    dot_general x10, matrix products, block_terms(): jnp.einsum('sqe,spe->sqp', query_tile, passage_tile, preferred_element_ty...  16.2 us
    another operation x1, loops' own time, shards(): slot_scores = lax.map(forward_block, offsets).reshape(owner_count, capacity)  9.92 us
  transfers between devices with their start and end apart: 6, of which 6 were waited for; matrix products, arithmetic and copies ran while one was open for 5% of the time, Pallas kernels for 0%

commit v1 on v0

--- a/solution.py
+++ b/solution.py
@@ -57,7 +57,8 @@
     send_code = slot_code.reshape(owner_count, capacity)
     sender = lax.iota(jnp.int32, slot_count) // capacity
     received_label = lax.all_to_all(send_code, "psg", split_axis=0, concat_axis=0, tiled=True)
-    query_rows = lax.all_gather(query_norm, "psg", axis=0, tiled=True)
+    sent = jnp.stack([query_norm] * lax.axis_size("psg"))
+    query_rows = jnp.concatenate(lax.all_to_all(sent, "psg", 0, 0), axis=0)
     flat_peek = received_label.reshape(-1)
     fetch_rows = sender * query_count + jnp.where(flat_peek > 0, (flat_peek - 1) // pass_count, 0)
     flat_code = received_label.reshape(-1)

time: 388 us -> 367 us (0.946)
  matrix products: 129 us -> 116 us
  waiting for transfers between devices: 140 us -> 127 us
    all_gather x1 -> x0, waiting for transfers between devices: 27.6 us -> none  [shards(): query_rows = lax.all_gather(query_norm, 'psg', axis=0, tiled=True)]
    all_to_all x0 -> x1, waiting for transfers between devices: none -> 12.8 us  [shards(): query_rows = jnp.concatenate(lax.all_to_all(sent, 'psg', 0, 0), axis=0)]
    dot_general x20, matrix products: 32.2 us -> 20 us  [select_rows(): jnp.dot(picker, flat_table, preferred_element_type=jnp.float32)]
    all_to_all x0 -> x1, starting transfers between devices: none -> 4.98 us  [shards(): query_rows = jnp.concatenate(lax.all_to_all(sent, 'psg', 0, 0), axis=0)]
where the time goes in v1:
time: 367 us; the launch traced here: 366 us
  waiting for transfers between devices  127 us (35%)
  matrix products  116 us (32%)
  local copies, waits for them, and re-layouts  54.2 us (15%)
  starting transfers between devices  22.7 us (6%)
  other arithmetic  20.2 us (6%)
  between operations  14.3 us (4%)
  loops' own time  10.6 us (3%)
    reduce_scatter x1, waiting for transfers between devices, shards(): lax.psum_scatter(query_accum.astype(jnp.bfloat16), 'psg', scatter_dimensi...  67.1 us
    dot_general x10, matrix products, add_rows(): jnp.einsum('sr,sx->rx', placer, flat_delta, precision=lax.Precision.HIGHEST)  66.4 us
    reduce_scatter x1, waiting for transfers between devices, shards(): lax.psum_scatter(passage_accum.astype(jnp.bfloat16), 'qry', scatter_dimen...  31.2 us
    while x60, local copies, waits for them, and re-layouts  31 us
    dot_general x20, matrix products, select_rows(): jnp.dot(picker, flat_table, preferred_element_type=jnp.float32)  20 us
    dot_general x10, matrix products, block_terms(): jnp.einsum('sqe,spe->sqp', query_tile, passage_tile, preferred_element_ty...  16.2 us
    all_to_all x1, waiting for transfers between devices, shards(): query_rows = jnp.concatenate(lax.all_to_all(sent, 'psg', 0, 0), axis=0)  12.8 us
    another operation x1, loops' own time, shards(): slot_scores = lax.map(forward_block, offsets).reshape(owner_count, capacity)  9.92 us
  transfers between devices with their start and end apart: 6, of which 6 were waited for; matrix products, arithmetic and copies ran while one was open for 5% of the time, Pallas kernels for 0%

profile of v1, /device:TPU:1, one launch (start us, length us, event | category | flops | bytes accessed | tf_op | source)
XLA Modules:
  0.0 365.6 jit_solution(2701382802776870042)
XLA Ops:
  10.3 9.6 %all-to-all-start = ((s32[32,1,10]{2,1,0:T(1,128)}), s32[32,1,10]{2,1,0:T(1,128)S(1)}, u32[]{:S(2)}, u32[]{:S(2)}) async-start(s32[32,1,10]{2,1,0:T(1,128)} %bitcast.4), calls=%async_computation | async-start | bytes 32768 | tf_op jit(solution)/shard_map/all_to_all | solution.py:59
  21.6 2.7 fusion.34
  28.0 5.0 %all-to-all-start.1 = ((bf16[32,4,32,128]{3,2,1,0:T(8,128)(2,1)}), bf16[32,4,32,128]{3,2,1,0:T(8,128)(2,1)S(1)}, u32[]{:S(2)}, u32[]{:S(2)}) async-start(bf16[32,4,32,128]{3,2,1,0:T(8,128)(2,1)} %stack.2), calls=%async_computation.1 | async-start | bytes 2097152 | tf_op jit(solution)/shard_map/all_to_all | solution.py:61
  33.0 3.8 %convert_multiply_fusion = (f32[32,256,128]{2,1,0:T(8,128)}, bf16[32,256,128]{2,1,0:T(8,128)(2,1)S(1)}) fusion(bf16[32,256,128]{2,1,0:T(8,128)(2,1)} %param.9, f32[32,256]{1,0:T(8,128)S(1)} %add_rsqrt_fusion), kind=kLoop, calls=%fused_computation.49 | loop fusion | flops 3145728 | bytes 8421376 | tf_op jit(solution)/shard_map/mul | solution.py:14
  37.1 12.8 %all-to-all-done.1 = bf16[32,4,32,128]{3,2,1,0:T(8,128)(2,1)S(1)} async-done(((bf16[32,4,32,128]{3,2,1,0:T(8,128)(2,1)}), bf16[32,4,32,128]{3,2,1,0:T(8,128)(2,1)S(1)}, u32[]{:S(2)}, u32[]{:S(2)}) %all-to-all-start.1) | async-done | bytes 1048608 | tf_op jit(solution)/shard_map/all_to_all | solution.py:61
  49.9 38.7 %while.27 = (s32[]{:T(128)}, f32[5,64]{1,0:T(8,128)S(1)}, s32[5]{0:T(128)S(1)}, s32[320]{0:T(512)S(1)}, bf16[32,4,32,128]{3,2,1,0:T(8,128)(2,1)S(1)}, /*index=5*...) while((s32[]{:T(128)}, f32[5,64]{1,0:T(8,128)S(1)}, ...), condition=%wide.region_9.10_spmd, body=%wide.region_6.9_spmd.sunk | while | flops 338964416 | bytes 22055336 | solution.py:87
  89.3 3.9 %all-to-all-start.2 = ((f32[32,1,10]{2,1,0:T(1,128)}), f32[32,1,10]{2,1,0:T(1,128)S(1)}, u32[]{:S(2)}, u32[]{:S(2)}) async-start(f32[32,1,10]{2,1,0:T(1,128)} %bitcast.5), calls=%async_computation.2 | async-start | bytes 32768 | tf_op jit(solution)/shard_map/all_to_all | solution.py:88
  93.4 6.8 %all-to-all-done.2 = f32[32,1,10]{2,1,0:T(1,128)S(1)} async-done(((f32[32,1,10]{2,1,0:T(1,128)}), f32[32,1,10]{2,1,0:T(1,128)S(1)}, u32[]{:S(2)}, u32[]{:S(2)}) %all-to-all-start.2) | async-done | bytes 1312 | tf_op jit(solution)/shard_map/all_to_all | solution.py:88
  104.8 4.1 %all-to-all-start.3 = ((f32[32,1,10]{2,1,0:T(1,128)}), f32[32,1,10]{2,1,0:T(1,128)S(1)}, u32[]{:S(2)}, u32[]{:S(2)}) async-start(f32[32,1,10]{2,1,0:T(1,128)} %bitcast.6), calls=%async_computation.3 | async-start | bytes 32768 | tf_op jit(solution)/shard_map/all_to_all | solution.py:100
  109.1 6.9 %all-to-all-done.3 = f32[32,1,10]{2,1,0:T(1,128)S(1)} async-done(((f32[32,1,10]{2,1,0:T(1,128)}), f32[32,1,10]{2,1,0:T(1,128)S(1)}, u32[]{:S(2)}, u32[]{:S(2)}) %all-to-all-start.3) | async-done | bytes 1312 | tf_op jit(solution)/shard_map/all_to_all | solution.py:100
  116.8 124.9 %while.28 = (s32[]{:T(128)}, f32[128,32,128]{2,0,1:T(8,128)}, f32[32,256,128]{2,0,1:T(8,128)}, s32[320]{0:T(512)S(1)}, f32[320]{0:T(512)S(1)}, /*index=5*/bf16[3...) while((s32[]{:T(128)}, f32[128,32,128]{2,0,1:T(8,128)}, ...), condition=%wide.region_15.16_spmd.clone, body=%wide.region_13.15_spmd.clone.sunk | while | flops 1822705664 | bytes 114847024 | solution.py:129
  123.7 2.6 select_add_fusion.4
  129.3 10.6 %select_add_fusion.5 = f32[32,256,128]{2,0,1:T(8,128)S(1)} fusion(f32[32,256,128]{2,0,1:T(8,128)S(1)} %copy-done, pred[]{:T(512)S(6)} %compare.11, s32[64]{0:T(128)S(1)} %dynamic_slice.59, f32[8,8,256,128]{3,2,1,0:T(8,128)S(1)} %bitcast.151), kind=kOutput, calls=%fused_computation.23.clone.1 | convolution fusion | flops 807405568 | bytes 16777472 | tf_op jit(solution)/shard_map/while/body/eval_jaxpr/sr,sx->rx/dot_general | solution.py:29
  148.7 2.6 select_add_fusion.4
  154.3 10.6 %select_add_fusion.5 = f32[32,256,128]{2,0,1:T(8,128)S(1)} fusion(f32[32,256,128]{2,0,1:T(8,128)S(1)} %copy-done, pred[]{:T(512)S(6)} %compare.11, s32[64]{0:T(128)S(1)} %dynamic_slice.59, f32[8,8,256,128]{3,2,1,0:T(8,128)S(1)} %bitcast.151), kind=kOutput, calls=%fused_computation.23.clone.1 | convolution fusion | flops 807405568 | bytes 16777472 | tf_op jit(solution)/shard_map/while/body/eval_jaxpr/sr,sx->rx/dot_general | solution.py:29
  179.2 10.6 %select_add_fusion.5 = f32[32,256,128]{2,0,1:T(8,128)S(1)} fusion(f32[32,256,128]{2,0,1:T(8,128)S(1)} %copy-done, pred[]{:T(512)S(6)} %compare.11, s32[64]{0:T(128)S(1)} %dynamic_slice.59, f32[8,8,256,128]{3,2,1,0:T(8,128)S(1)} %bitcast.151), kind=kOutput, calls=%fused_computation.23.clone.1 | convolution fusion | flops 807405568 | bytes 16777472 | tf_op jit(solution)/shard_map/while/body/eval_jaxpr/sr,sx->rx/dot_general | solution.py:29
  204.1 10.6 %select_add_fusion.5 = f32[32,256,128]{2,0,1:T(8,128)S(1)} fusion(f32[32,256,128]{2,0,1:T(8,128)S(1)} %copy-done, pred[]{:T(512)S(6)} %compare.11, s32[64]{0:T(128)S(1)} %dynamic_slice.59, f32[8,8,256,128]{3,2,1,0:T(8,128)S(1)} %bitcast.151), kind=kOutput, calls=%fused_computation.23.clone.1 | convolution fusion | flops 807405568 | bytes 16777472 | tf_op jit(solution)/shard_map/while/body/eval_jaxpr/sr,sx->rx/dot_general | solution.py:29
  223.5 2.6 select_add_fusion.4
  229.1 10.6 %select_add_fusion.5 = f32[32,256,128]{2,0,1:T(8,128)S(1)} fusion(f32[32,256,128]{2,0,1:T(8,128)S(1)} %copy-done, pred[]{:T(512)S(6)} %compare.11, s32[64]{0:T(128)S(1)} %dynamic_slice.59, f32[8,8,256,128]{3,2,1,0:T(8,128)S(1)} %bitcast.151), kind=kOutput, calls=%fused_computation.23.clone.1 | convolution fusion | flops 807405568 | bytes 16777472 | tf_op jit(solution)/shard_map/while/body/eval_jaxpr/sr,sx->rx/dot_general | solution.py:29
  241.7 3.8 %copy.86 = bf16[128,32,128]{2,1,0:T(8,128)(2,1)} copy(f32[128,32,128]{2,0,1:T(8,128)} %get-tuple-element.205) | data formatting | bytes 3145728 | tf_op jit(solution)/shard_map/while | solution.py:129
  245.5 6.0 %copy.85 = bf16[32,256,128]{2,1,0:T(8,128)(2,1)} copy(f32[32,256,128]{2,0,1:T(8,128)} %get-tuple-element.206) | data formatting | bytes 6291456 | tf_op jit(solution)/shard_map/while | solution.py:129
  252.2 67.1 %reduce-scatter.3.cloned.1.call-done = bf16[4,32,128]{2,1,0:T(8,128)(2,1)} async-done(((bf16[128,32,128]{2,1,0:T(8,128)(2,1)}), bf16[4,32,128]{2,1,0:T(8,128)(2,1)}) %reduce-scatter.3.cloned.1.call-update) | async-done | bytes 32784 | tf_op jit(solution)/shard_map/reduce_scatter | solution.py:130
  321.2 31.2 %reduce-scatter.5.cloned.1.call-done = bf16[32,64,128]{2,1,0:T(8,128)(2,1)} async-done(((bf16[32,256,128]{2,1,0:T(8,128)(2,1)}), bf16[32,64,128]{2,1,0:T(8,128)(2,1)}) %reduce-scatter.5.cloned.1.call-update) | async-done | bytes 524304 | tf_op jit(solution)/shard_map/reduce_scatter | solution.py:133
  352.4 6.3 %fusion.39 = bf16[32,64,128]{2,1,0:T(8,128)(2,1)} fusion(bf16[32,64,128]{2,1,0:T(8,128)(2,1)} %reduce-scatter.5.cloned.1.call-done, f32[32,256,128]{2,1,0:T(8,128)} %get-tuple-element.270, s32[]{:T(128)S(6)} %select_n.80, f32[32,64]{1,0:T(8,128)S(1)} %constant_dynamic-slice_fusion), kind=kOutput, calls=%fused_computation.59 | output fusion | flops 1837183 | bytes 3679232 | tf_op jit(solution)/shard_map/mul | solution.py:144
  (200 shorter events, 109.7 us)
Async XLA Ops:
  10.3 16.5 %all-to-all-start = ((s32[32,1,10]{2,1,0:T(1,128)}), s32[32,1,10]{2,1,0:T(1,128)S(1)}, u32[]{:S(2)}, u32[]{:S(2)}) async-start(s32[32,1,10]{2,1,0:T(1,128)} %bitcast.4), calls=%async_computation | async-start | bytes 32768 | tf_op jit(solution)/shard_map/all_to_all | solution.py:59
  28.0 21.9 %all-to-all-start.1 = ((bf16[32,4,32,128]{3,2,1,0:T(8,128)(2,1)}), bf16[32,4,32,128]{3,2,1,0:T(8,128)(2,1)S(1)}, u32[]{:S(2)}, u32[]{:S(2)}) async-start(bf16[32,4,32,128]{3,2,1,0:T(8,128)(2,1)} %stack.2), calls=%async_computation.1 | async-start | bytes 2097152 | tf_op jit(solution)/shard_map/all_to_all | solution.py:61
  49.9 43.3 %copy-start.5 = (f32[4,32]{1,0:T(4,128)S(1)}, f32[4,32]{1,0:T(4,128)}, u32[]{:S(2)}) copy-start(f32[4,32]{1,0:T(4,128)} %param.11) | copy-start | bytes 1540
  89.3 10.8 %all-to-all-start.2 = ((f32[32,1,10]{2,1,0:T(1,128)}), f32[32,1,10]{2,1,0:T(1,128)S(1)}, u32[]{:S(2)}, u32[]{:S(2)}) async-start(f32[32,1,10]{2,1,0:T(1,128)} %bitcast.5), calls=%async_computation.2 | async-start | bytes 32768 | tf_op jit(solution)/shard_map/all_to_all | solution.py:88
  104.8 11.2 %all-to-all-start.3 = ((f32[32,1,10]{2,1,0:T(1,128)}), f32[32,1,10]{2,1,0:T(1,128)S(1)}, u32[]{:S(2)}, u32[]{:S(2)}) async-start(f32[32,1,10]{2,1,0:T(1,128)} %bitcast.6), calls=%async_computation.3 | async-start | bytes 32768 | tf_op jit(solution)/shard_map/all_to_all | solution.py:100
  109.0 210.3 %reduce-scatter.3.cloned.1.call-start = ((), (), s32[]{:S(2)}) async-start(), calls=%async_computation.6 | async-start | bytes 1081344 | tf_op jit(solution)/shard_map/reduce_scatter | solution.py:130
  122.1 1.6 copy-start.2
  126.4 1.9 copy-start.3
  126.4 2.9 copy-start
  140.0 2.0 copy-start.1
  151.3 1.9 copy-start.3
  151.3 2.9 copy-start
  164.9 2.0 copy-start.1
  176.2 1.9 copy-start.3
  176.3 2.9 copy-start
  189.8 2.0 copy-start.1
  201.2 1.9 copy-start.3
  201.2 2.9 copy-start
  214.8 2.0 copy-start.1
  226.1 1.9 copy-start.3
  226.1 2.9 copy-start
  239.7 2.0 copy-start.1
  245.5 106.9 %reduce-scatter.5.cloned.1.call-start = ((), (), s32[]{:S(2)}) async-start(), calls=%async_computation.7 | async-start | bytes 2621440 | tf_op jit(solution)/shard_map/reduce_scatter | solution.py:133
  251.5 67.7 %copy-start.4 = (bf16[4,32,128]{2,1,0:T(8,128)(2,1)S(1)}, bf16[4,32,128]{2,1,0:T(8,128)(2,1)}, u32[]{:S(2)}) copy-start(bf16[4,32,128]{2,1,0:T(8,128)(2,1)} %param.8) | copy-start | bytes 98308
  (4 other events, 6.4 us)
Sparse Core Ops, SparseCore 0:
  245.6 73.6 reduce-scatter.2
  321.7 30.7 reduce-scatter.4
